TPU v7x, 32 devices: a whole 2x2x4 slice. The times are simulated.
32 devices in a mesh: tile: 8 (over z, y), src: 4 (over x, core).
Axes of the slice: x: 2, y: 2, z: 4, core: 2. Of those that a mesh axis runs over, the one named last changes fastest.
Arguments:
- excitation: bfloat16 [2, 512, 8192], P(None, 'src', 'tile'), may hold values from -6 to 6
- near_blocks: bfloat16 [16, 3, 2, 512, 512], P('tile'), may hold values from -0.02734375 to 0.02734375
- source_basis: bfloat16 [16, 2, 24, 512], P('tile'), may hold values from -0.1875 to 0.1875
- target_basis: bfloat16 [16, 2, 24, 512], P('tile'), may hold values from -0.625 to 0.625
- coupling: bfloat16 [2, 384, 384], P(None, None, 'tile'), may hold values from -0.109375 to 0.109375
- pair_rank: int32 [16, 16], P(None, 'tile'), may hold values from 2 to 24
- far_link: int32 [16, 16], P(None, 'tile'), may hold values 0 or 1
- focal_kernel: bfloat16 [2, 64, 8192], P(None, None, 'tile'), may hold values from -0.046875 to 0.046875
- focal_target: float32 [64], replicated, may hold values from 0.3 to 0.9
- focal_owner: int32 [64], replicated, may hold values from 0 to 63, each once
Outputs:
- field: float32 [2, 512, 8192], P(None, 'src', 'tile')
- focal_residual: float32 [64], P('tile')
- adjoint: float32 [2, 512, 8192], P(None, 'src', 'tile')
Inputs may be any that keep to these rules, and one draw needn't show every extreme that they name: `focal_owner`: each focal point has its own slot; slot k belongs to index k // 8 of tile.
All inputs are finite; a program needn't handle non-finite values. No bound on the sum of `far_link` on one device may be relied on, other than what follows from the above.
Results may differ from a plain program's by a relative error of at most 0.006.
Values may be sent and summed in bfloat16 or wider, within the bound.
No kernel may reach another device: no remote copies, remote signals or barrier semaphores. Data moves between devices by JAX's collectives and lax.ppermute only.
A program may use at most 64 MiB of HBM per device.

v0:
```python
import jax
import jax.numpy as jnp
from jax import lax
from jax.sharding import PartitionSpec as P

TILE = 512
RANK = 24
DAMPING = 0.8


def extended(x, sides, width):
    for axis, dim in sides:
        size, length = (lax.axis_size(axis), x.shape[dim])
        up = [(i, (i + 1) % size) for i in range(size)]
        down = [(j, i) for i, j in up]
        last = lax.slice_in_dim(x, length - width, length, axis=dim)
        initial = lax.slice_in_dim(x, 0, width, axis=dim)
        before = lax.ppermute(last, axis, up)
        after = lax.ppermute(initial, axis, down)
        x = jnp.concatenate([before, x, after], axis=dim)
    return x


def plain_dot(left, right, contract):
    return lax.dot_general(
        left, right, (((1,), (contract,)), ((), ())), preferred_element_type=jnp.float32
    )


def complex_dot(left_re, left_im, right_re, right_im, contract):
    real_part = plain_dot(left_re, right_re, contract) - plain_dot(left_im, right_im, contract)
    imag_part = plain_dot(left_re, right_im, contract) + plain_dot(left_im, right_re, contract)
    return (real_part, imag_part)


def per_device(
    excitation,
    near_blocks,
    source_basis,
    target_basis,
    coupling,
    pair_rank,
    far_link,
    focal_kernel,
    focal_target,
    focal_owner,
):
    tile_count = near_blocks.shape[0]
    src_rows = excitation.shape[1]
    tiles = pair_rank.shape[0]
    focal_count = focal_target.shape[0]
    first_tile = lax.axis_index("tile") * tile_count
    global_tiles = first_tile + jnp.arange(tile_count)
    source_tiles = jnp.arange(tiles)[:, None]
    distance = (global_tiles[None, :] - source_tiles) % tiles
    far_pairs = (far_link == 1) & (distance != 0) & (distance != 1) & (distance != tiles - 1)
    levels = jnp.arange(RANK)
    rank_limit = pair_rank[:, None, :, None]
    rank_mask = (
        far_pairs[:, None, :, None]
        & (levels[None, :, None, None] < rank_limit)
        & (levels[None, None, None, :] < rank_limit)
    )
    rank_mask = rank_mask.reshape(tiles * RANK, tile_count * RANK)
    masked = coupling * rank_mask.astype(coupling.dtype)
    flipped = lax.all_to_all(masked, "tile", split_axis=1, concat_axis=2, tiled=True)

    def apply_transpose(field):
        field_bf = field.astype(jnp.bfloat16)
        moved_re = [[], [], []]
        moved_im = [[], [], []]
        proj_re = []
        proj_im = []
        for tile_here in range(tile_count):
            own = field_bf[:, :, tile_here * TILE : (tile_here + 1) * TILE]
            for offset in range(3):
                part_re, part_im = complex_dot(
                    own[0],
                    own[1],
                    near_blocks[tile_here, offset, 0],
                    near_blocks[tile_here, offset, 1],
                    1,
                )
                moved_re[offset].append(part_re)
                moved_im[offset].append(part_im)
            part_re, part_im = complex_dot(
                own[0], own[1], target_basis[tile_here, 0], target_basis[tile_here, 1], 1
            )
            proj_re.append(part_re)
            proj_im.append(part_im)
        moved = [
            jnp.stack([jnp.concatenate(moved_re[k], axis=1), jnp.concatenate(moved_im[k], axis=1)])
            for k in range(3)
        ]
        width = tile_count * TILE
        edges = jnp.concatenate([moved[0][:, :, 0:TILE], moved[2][:, :, width - TILE :]], axis=2)
        arrived = extended(edges.astype(jnp.bfloat16), (("tile", 2),), TILE).astype(edges.dtype)
        from_left = jnp.concatenate(
            [arrived[:, :, 0:TILE], moved[2][:, :, 0 : width - TILE]], axis=2
        )
        from_right = jnp.concatenate(
            [moved[0][:, :, TILE:], arrived[:, :, 3 * TILE : 4 * TILE]], axis=2
        )
        near_part = moved[1] + from_left + from_right
        projected = jnp.stack(
            [jnp.concatenate(proj_re, axis=1), jnp.concatenate(proj_im, axis=1)]
        ).astype(jnp.bfloat16)
        shard_piece = lax.all_gather(projected, "tile", axis=2, tiled=True)
        term_re, term_im = complex_dot(shard_piece[0], shard_piece[1], flipped[0], flipped[1], 1)
        summed_back = jnp.stack([term_re, term_im]).astype(jnp.bfloat16)
        far_re = []
        far_im = []
        for tile_here in range(tile_count):
            piece = summed_back[:, :, tile_here * RANK : (tile_here + 1) * RANK]
            part_re, part_im = complex_dot(
                piece[0], piece[1], source_basis[tile_here, 0], source_basis[tile_here, 1], 0
            )
            far_re.append(part_re)
            far_im.append(part_im)
        far_part = jnp.stack([jnp.concatenate(far_re, axis=1), jnp.concatenate(far_im, axis=1)])
        return field + near_part + far_part

    right_side = excitation.astype(jnp.float32)
    field = right_side
    for update in range(2):
        apply_field_bf = field.astype(jnp.bfloat16)
        padded = extended(apply_field_bf, (("tile", 2),), TILE)
        coeff_re = []
        coeff_im = []
        for apply_tile_here in range(tile_count):
            apply_own = apply_field_bf[:, :, apply_tile_here * TILE : (apply_tile_here + 1) * TILE]
            apply_part_re, apply_part_im = complex_dot(
                apply_own[0],
                apply_own[1],
                source_basis[apply_tile_here, 0],
                source_basis[apply_tile_here, 1],
                1,
            )
            coeff_re.append(apply_part_re)
            coeff_im.append(apply_part_im)
        coeff = jnp.stack(
            [jnp.concatenate(coeff_re, axis=1), jnp.concatenate(coeff_im, axis=1)]
        ).astype(jnp.bfloat16)
        fold_shard_piece = lax.all_gather(coeff, "tile", axis=2, tiled=True)
        fold_term_re, fold_term_im = complex_dot(
            fold_shard_piece[0], fold_shard_piece[1], masked[0], masked[1], 0
        )
        coupled = jnp.stack([fold_term_re, fold_term_im]).astype(jnp.bfloat16)
        out_re = []
        out_im = []
        for apply_tile_here in range(tile_count):
            total_re = jnp.zeros((src_rows, TILE), jnp.float32)
            total_im = jnp.zeros((src_rows, TILE), jnp.float32)
            for apply_offset in range(3):
                window = padded[
                    :,
                    :,
                    (apply_tile_here + apply_offset)
                    * TILE : (apply_tile_here + apply_offset + 1)
                    * TILE,
                ]
                apply_part_re, apply_part_im = complex_dot(
                    window[0],
                    window[1],
                    near_blocks[apply_tile_here, apply_offset, 0],
                    near_blocks[apply_tile_here, apply_offset, 1],
                    0,
                )
                total_re = total_re + apply_part_re
                total_im = total_im + apply_part_im
            apply_piece = coupled[:, :, apply_tile_here * RANK : (apply_tile_here + 1) * RANK]
            apply_part_re, apply_part_im = complex_dot(
                apply_piece[0],
                apply_piece[1],
                target_basis[apply_tile_here, 0],
                target_basis[apply_tile_here, 1],
                0,
            )
            out_re.append(total_re + apply_part_re)
            out_im.append(total_im + apply_part_im)
        added = jnp.stack([jnp.concatenate(out_re, axis=1), jnp.concatenate(out_im, axis=1)])
        field = field + DAMPING * (right_side - (field + added))
    field_bf = field.astype(jnp.bfloat16)
    focal_re, focal_im = complex_dot(field_bf[0], field_bf[1], focal_kernel[0], focal_kernel[1], 1)
    slots_here = focal_count // lax.axis_size("tile")
    first_slot = lax.axis_index("tile") * slots_here
    sources = src_rows * lax.axis_size("src")
    permute = (focal_owner[:, None] == jnp.arange(focal_count)[None, :]).astype(jnp.float32)
    summed_focal = lax.psum(jnp.stack([focal_re, focal_im]), "tile")
    intensity = lax.psum(
        jnp.sum(summed_focal[0] * summed_focal[0] + summed_focal[1] * summed_focal[1], axis=0),
        "src",
    )
    residual_part = jnp.tanh(intensity / (2.0 * sources)) - focal_target
    weights_re = (residual_part * summed_focal[0]).astype(jnp.bfloat16)
    weights_im = (-residual_part * summed_focal[1]).astype(jnp.bfloat16)
    residual_slots = jnp.dot(residual_part, permute, precision=lax.Precision.HIGHEST)
    residual_out = lax.dynamic_slice_in_dim(residual_slots, first_slot, slots_here)
    scale_factor = (tiles * TILE / focal_count) ** 0.5
    term_re, term_im = complex_dot(weights_re, weights_im, focal_kernel[0], focal_kernel[1], 0)
    source_term = jnp.stack([term_re, term_im]) * scale_factor
    adjoint = source_term + DAMPING * (source_term - apply_transpose(source_term))
    return (field, residual_out, adjoint)


def solution(mesh):
    return jax.shard_map(
        per_device,
        mesh=mesh,
        in_specs=(
            P(None, "src", "tile"),
            P("tile", None, None, None, None),
            P("tile", None, None, None),
            P("tile", None, None, None),
            P(None, None, "tile"),
            P(None, "tile"),
            P(None, "tile"),
            P(None, None, "tile"),
            P(),
            P(),
        ),
        out_specs=(P(None, "src", "tile"), P("tile"), P(None, "src", "tile")),
        check_vma=False,
    )
```

profile of v0, /device:TPU:0, one launch (start us, length us, event | category | flops | bytes accessed | tf_op | source)
XLA Modules:
  0.0 293.0 jit_solution(17563514672564382302)
XLA Ops:
  7.2 2.0 fusion.459
  9.1 6.0 %collective-permute-start.1 = (bf16[2,128,512]{2,1,0:T(8,128)(2,1)}, bf16[2,128,512]{2,1,0:T(8,128)(2,1)}, u32[]{:S(2)}, u32[]{:S(2)}) collective-permute-start(bf16[2,128,512]{2,1,0:T(8,128)(2,1)} %get-tuple-element.12), channel_id=1, source_target_pairs={{4,0},{8,4},{12,8},{16,12},{20,16},{24,20},{28,24},{0,28},{5,1},{9... | collective-permute-start | bytes 786440 | tf_op jit(solution)/shard_map/ppermute | solution.py:19
  19.8 6.0 %all-to-all-start = ((bf16[8,2,2304]{2,1,0:T(2,128)(2,1)}), bf16[8,2,2304]{2,1,0:T(2,128)(2,1)S(1)}, u32[]{:S(2)}, u32[]{:S(2)}) async-start(bf16[8,2,2304]{2,1,0:T(2,128)(2,1)} %reshape.84), calls=%async_computation | async-start | bytes 147456 | tf_op jit(solution)/shard_map/all_to_all | solution.py:66
  34.8 31.3 %all_gather.9 = bf16[2,128,384]{1,2,0:T(8,128)(2,1)S(1)} all-gather(bf16[2,128,48]{1,2,0:T(8,128)(2,1)S(1)} %pad_maximum_fusion.6), channel_id=1, replica_groups=mesh['tile'=8,'src'=4] {'tile'}, dimensions={2}, use_global_device_ids=true | all-gather | bytes 221184 | tf_op jit(solution)/shard_map/all_gather | solution.py:144
  66.3 1.3 fusion.94
  67.7 1.3 fusion.112
  84.3 1.8 fusion.85
  86.1 1.3 fusion.175
  87.4 1.5 fusion.20
  88.9 1.5 fusion.22
  90.5 1.3 fusion.77
  96.9 30.7 %all_gather.10 = bf16[2,128,384]{1,2,0:T(8,128)(2,1)S(1)} all-gather(bf16[2,128,48]{1,2,0:T(8,128)(2,1)S(1)} %pad_maximum_fusion.7), channel_id=1, replica_groups=mesh['tile'=8,'src'=4] {'tile'}, dimensions={2}, use_global_device_ids=true | all-gather | bytes 221184 | tf_op jit(solution)/shard_map/all_gather | solution.py:144
  131.0 4.0 %collective-permute-start.3 = (bf16[2,128,512]{2,1,0:T(8,128)(2,1)S(1)}, bf16[2,128,512]{2,1,0:T(8,128)(2,1)S(1)}, u32[]{:S(2)}, u32[]{:S(2)}) collective-permute-start(bf16[2,128,512]{2,1,0:T(8,128)(2,1)S(1)} %get-tuple-element.10), channel_id=1, source_target_pairs={{4,0},{8,4},{12,8},{16,12},{20,16},{24,20},{28,24},{0,28},{5,1},{9... | collective-permute-start | bytes 786440 | tf_op jit(solution)/shard_map/ppermute | solution.py:19
  139.2 5.9 %collective-permute-done.2 = bf16[2,128,512]{2,1,0:T(8,128)(2,1)S(1)} collective-permute-done((bf16[2,128,512]{2,1,0:T(8,128)(2,1)S(1)}, bf16[2,128,512]{2,1,0:T(8,128)(2,1)S(1)}, u32[]{:S(2)}, u32[]{:S(2)}) %collective-permute-start.2) | collective-permute-done | bytes 262176 | tf_op jit(solution)/shard_map/ppermute | solution.py:18
  150.1 66.4 %all-reduce.2.cloned.1.call-done = f32[2,128,64]{1,2,0:T(8,128)} async-done(((f32[2,128,64]{1,2,0:T(8,128)}), f32[2,128,64]{1,2,0:T(8,128)}) %all-reduce.2.cloned.1.call-update) | async-done | bytes 65552 | tf_op jit(solution)/shard_map/psum | solution.py:189
  217.4 5.8 %psum.15 = f32[64]{0:T(128)S(1)} all-reduce(f32[64]{0:T(128)S(1)} %add_reduce_fusion), channel_id=1, replica_groups=mesh['tile'=8,'src'=4] {'src'}, use_global_device_ids=true, to_apply=%region_2.3 | all-reduce | flops 64 | bytes 512 | tf_op jit(solution)/shard_map/psum | solution.py:190
  227.9 1.3 fusion.106
  229.2 1.4 fusion.160
  230.6 1.3 fusion.116
  236.1 30.7 %all_gather.11 = bf16[2,128,384]{1,2,0:T(8,128)(2,1)S(1)} all-gather(bf16[2,128,48]{1,2,0:T(8,128)(2,1)S(1)} %pad_maximum_fusion.8), channel_id=1, replica_groups=mesh['tile'=8,'src'=4] {'tile'}, dimensions={2}, use_global_device_ids=true | all-gather | bytes 221184 | tf_op jit(solution)/shard_map/all_gather | solution.py:108
  272.0 3.3 %collective-permute-start.5 = (bf16[2,128,512]{2,1,0:T(8,128)(2,1)S(1)}, bf16[2,128,512]{2,1,0:T(8,128)(2,1)S(1)}, u32[]{:S(2)}, u32[]{:S(2)}) collective-permute-start(bf16[2,128,512]{2,1,0:T(8,128)(2,1)S(1)} %fusion.67), channel_id=1, source_target_pairs={{4,0},{8,4},{12,8},{16,12},{20,16},{24,20},{28,24},{0,28},{5,1},{9... | collective-permute-start | bytes 786440 | tf_op jit(solution)/shard_map/ppermute | solution.py:19
  277.4 2.2 collective-permute-done.5
  279.7 4.8 %collective-permute-done.4 = bf16[2,128,512]{2,1,0:T(8,128)(2,1)S(1)} collective-permute-done((bf16[2,128,512]{2,1,0:T(8,128)(2,1)S(1)}, bf16[2,128,512]{2,1,0:T(8,128)(2,1)S(1)}, u32[]{:S(2)}, u32[]{:S(2)}) %collective-permute-start.4) | collective-permute-done | bytes 262176 | tf_op jit(solution)/shard_map/ppermute | solution.py:18
  284.6 1.6 fusion.61
  (219 shorter events, 62.8 us)
Async XLA Ops:
  7.2 62.5 %copy-start.1 = (bf16[2,128,1024]{2,1,0:T(8,128)(2,1)S(1)}, bf16[2,128,1024]{2,1,0:T(8,128)(2,1)}, u32[]{:S(2)}) copy-start(bf16[2,128,1024]{2,1,0:T(8,128)(2,1)} %param.10) | copy-start | bytes 1572868
  7.2 62.0 %copy-start.2 = (bf16[2,2,24,512]{3,2,1,0:T(8,128)(2,1)S(1)}, bf16[2,2,24,512]{3,2,1,0:T(8,128)(2,1)}, u32[]{:S(2)}) copy-start(bf16[2,2,24,512]{3,2,1,0:T(8,128)(2,1)} %param.13) | copy-start | bytes 294916
  9.1 75.1 %collective-permute-start.1 = (bf16[2,128,512]{2,1,0:T(8,128)(2,1)}, bf16[2,128,512]{2,1,0:T(8,128)(2,1)}, u32[]{:S(2)}, u32[]{:S(2)}) collective-permute-start(bf16[2,128,512]{2,1,0:T(8,128)(2,1)} %get-tuple-element.12), channel_id=1, source_target_pairs={{4,0},{8,4},{12,8},{16,12},{20,16},{24,20},{28,24},{0,28},{5,1},{9... | collective-permute-start | bytes 786440 | tf_op jit(solution)/shard_map/ppermute | solution.py:19
  15.2 70.9 %collective-permute-start = (bf16[2,128,512]{2,1,0:T(8,128)(2,1)}, bf16[2,128,512]{2,1,0:T(8,128)(2,1)}, u32[]{:S(2)}, u32[]{:S(2)}) collective-permute-start(bf16[2,128,512]{2,1,0:T(8,128)(2,1)} %get-tuple-element.11), channel_id=1, source_target_pairs={{0,4},{4,8},{8,12},{12,16},{16,20},{20,24},{24,28},{28,0},{1,5},{5... | collective-permute-start | bytes 786440 | tf_op jit(solution)/shard_map/ppermute | solution.py:18
  19.8 62.4 %all-to-all-start = ((bf16[8,2,2304]{2,1,0:T(2,128)(2,1)}), bf16[8,2,2304]{2,1,0:T(2,128)(2,1)S(1)}, u32[]{:S(2)}, u32[]{:S(2)}) async-start(bf16[8,2,2304]{2,1,0:T(2,128)(2,1)} %reshape.84), calls=%async_computation | async-start | bytes 147456 | tf_op jit(solution)/shard_map/all_to_all | solution.py:66
  25.8 190.7 %all-reduce.2.cloned.1.call-start = ((), (), s32[]{:S(2)}) async-start(), calls=%async_computation.1 | async-start | bytes 131072 | tf_op jit(solution)/shard_map/psum | solution.py:189
  25.8 46.6 %copy-start = (bf16[2,3,2,512,512]{4,3,2,1,0:T(8,128)(2,1)S(1)}, bf16[2,3,2,512,512]{4,3,2,1,0:T(8,128)(2,1)}, u32[]{:S(2)}) copy-start(bf16[2,3,2,512,512]{4,3,2,1,0:T(8,128)(2,1)} %param.11) | copy-start | bytes 18874372
  77.7 14.1 %slice-start = ((s8[6291456]{0:T(1024)(128)(4,1)}), s8[2097152]{0:T(1024)(128)(4,1)S(1)}, s32[]{:S(2)}) async-start(s8[6291456]{0:T(1024)(128)(4,1)} %bitcast.613), calls=%async_computation.2 | async-start | bytes 4194304
  83.1 9.9 %copy-start.6 = (f32[128,512]{1,0:T(8,128)S(1)}, f32[128,512]{1,0:T(8,128)}, u32[]{:S(2)}) copy-start(f32[128,512]{1,0:T(8,128)} %convolution_subtract_fusion.23) | copy-start | bytes 786436
  83.1 9.9 %copy-start.7 = (f32[128,512]{1,0:T(8,128)S(1)}, f32[128,512]{1,0:T(8,128)}, u32[]{:S(2)}) copy-start(f32[128,512]{1,0:T(8,128)} %fusion.3) | copy-start | bytes 786436
  83.1 11.1 %copy-start.4 = (f32[128,512]{1,0:T(8,128)S(1)}, f32[128,512]{1,0:T(8,128)}, u32[]{:S(2)}) copy-start(f32[128,512]{1,0:T(8,128)} %convolution_subtract_fusion.16) | copy-start | bytes 786436
  83.1 11.1 %copy-start.5 = (f32[128,512]{1,0:T(8,128)S(1)}, f32[128,512]{1,0:T(8,128)}, u32[]{:S(2)}) copy-start(f32[128,512]{1,0:T(8,128)} %convolution_subtract_fusion.17) | copy-start | bytes 786436
  83.1 8.8 %slice-start.1 = ((s8[6291456]{0:T(1024)(128)(4,1)}), s8[4194304]{0:T(1024)(128)(4,1)S(1)}, s32[]{:S(2)}) async-start(s8[6291456]{0:T(1024)(128)(4,1)} %bitcast.613), calls=%async_computation.3 | async-start | bytes 8388608
  87.4 8.2 %copy-start.8 = (bf16[2,2,24,512]{3,2,1,0:T(8,128)(2,1)S(1)}, bf16[2,2,24,512]{3,2,1,0:T(8,128)(2,1)}, u32[]{:S(2)}) copy-start(bf16[2,2,24,512]{3,2,1,0:T(8,128)(2,1)} %param.12) | copy-start | bytes 294916
  131.0 7.9 %collective-permute-start.3 = (bf16[2,128,512]{2,1,0:T(8,128)(2,1)S(1)}, bf16[2,128,512]{2,1,0:T(8,128)(2,1)S(1)}, u32[]{:S(2)}, u32[]{:S(2)}) collective-permute-start(bf16[2,128,512]{2,1,0:T(8,128)(2,1)S(1)} %get-tuple-element.10), channel_id=1, source_target_pairs={{4,0},{8,4},{12,8},{16,12},{20,16},{24,20},{28,24},{0,28},{5,1},{9... | collective-permute-start | bytes 786440 | tf_op jit(solution)/shard_map/ppermute | solution.py:19
  136.0 9.1 %collective-permute-start.2 = (bf16[2,128,512]{2,1,0:T(8,128)(2,1)S(1)}, bf16[2,128,512]{2,1,0:T(8,128)(2,1)S(1)}, u32[]{:S(2)}, u32[]{:S(2)}) collective-permute-start(bf16[2,128,512]{2,1,0:T(8,128)(2,1)S(1)} %get-tuple-element.9), channel_id=1, source_target_pairs={{0,4},{4,8},{8,12},{12,16},{16,20},{20,24},{24,28},{28,0},{1,5},{5... | collective-permute-start | bytes 786440 | tf_op jit(solution)/shard_map/ppermute | solution.py:18
  145.9 2.4 copy-start.3
  146.2 77.1 %copy-start.10 = (f32[64]{0:T(128)S(1)}, f32[64]{0:T(128)}, u32[]{:S(2)}) copy-start(f32[64]{0:T(128)} %param.18) | copy-start | bytes 772
  147.0 85.0 %slice-start.2 = ((s8[6291456]{0:T(1024)(128)(4,1)}), s8[2097152]{0:T(1024)(128)(4,1)S(1)}, s32[]{:S(2)}) async-start(s8[6291456]{0:T(1024)(128)(4,1)} %bitcast.615), calls=%async_computation.4 | async-start | bytes 4194304
  223.2 8.7 %slice-start.3 = ((s8[6291456]{0:T(1024)(128)(4,1)}), s8[4194304]{0:T(1024)(128)(4,1)S(1)}, s32[]{:S(2)}) async-start(s8[6291456]{0:T(1024)(128)(4,1)} %bitcast.615), calls=%async_computation.5 | async-start | bytes 8388608
  229.2 38.0 %copy-start.9 = (bf16[2,2,24,512]{3,2,1,0:T(8,128)(2,1)S(1)}, bf16[2,2,24,512]{3,2,1,0:T(8,128)(2,1)}, u32[]{:S(2)}) copy-start(bf16[2,2,24,512]{3,2,1,0:T(8,128)(2,1)} %param.12) | copy-start | bytes 294916
  271.5 5.0 %copy-start.11 = (s32[64]{0:T(128)S(1)}, s32[64]{0:T(128)}, u32[]{:S(2)}) copy-start(s32[64]{0:T(128)} %param.19) | copy-start | bytes 772
  272.0 7.7 %collective-permute-start.5 = (bf16[2,128,512]{2,1,0:T(8,128)(2,1)S(1)}, bf16[2,128,512]{2,1,0:T(8,128)(2,1)S(1)}, u32[]{:S(2)}, u32[]{:S(2)}) collective-permute-start(bf16[2,128,512]{2,1,0:T(8,128)(2,1)S(1)} %fusion.67), channel_id=1, source_target_pairs={{4,0},{8,4},{12,8},{16,12},{20,16},{24,20},{28,24},{0,28},{5,1},{9... | collective-permute-start | bytes 786440 | tf_op jit(solution)/shard_map/ppermute | solution.py:19
  275.4 9.1 %collective-permute-start.4 = (bf16[2,128,512]{2,1,0:T(8,128)(2,1)S(1)}, bf16[2,128,512]{2,1,0:T(8,128)(2,1)S(1)}, u32[]{:S(2)}, u32[]{:S(2)}) collective-permute-start(bf16[2,128,512]{2,1,0:T(8,128)(2,1)S(1)} %fusion.69), channel_id=1, source_target_pairs={{0,4},{4,8},{8,12},{12,16},{16,20},{20,24},{24,28},{28,0},{1,5},{5... | collective-permute-start | bytes 786440 | tf_op jit(solution)/shard_map/ppermute | solution.py:18
Sparse Core Ops, SparseCore 0:
  150.0 66.4 all-reduce.1
where the time goes:
time: 294 us; the launch traced here: 293 us
  blocking collectives  98.5 us (34%)
  waiting for transfers between devices  80.4 us (27%)
  matrix products  64.3 us (22%)
  starting transfers between devices  19.5 us (7%)
  between operations  15.3 us (5%)
  other arithmetic  8.67 us (3%)
  local copies, waits for them, and re-layouts  6.31 us (2%)
    psum x1, waiting for transfers between devices, per_device(): summed_focal = lax.psum(jnp.stack([focal_re, focal_im]), 'tile')  66.4 us
    dot_general x140, matrix products, plain_dot(): lax.dot_general(left, right, (((1,), (contract,)), ((), ())), preferred_e...  64.1 us
    all_gather x2, blocking collectives, per_device(): fold_shard_piece = lax.all_gather(coeff, 'tile', axis=2, tiled=True)  62 us
    all_gather x1, blocking collectives, apply_transpose(): shard_piece = lax.all_gather(projected, 'tile', axis=2, tiled=True)  30.7 us
    ppermute x3, starting transfers between devices, extended(): after = lax.ppermute(initial, axis, down)  13.3 us
    ppermute x3, waiting for transfers between devices, extended(): before = lax.ppermute(last, axis, up)  10.7 us
    all_to_all x1, starting transfers between devices, per_device(): lax.all_to_all(masked, 'tile', split_axis=1, concat_axis=2, tiled=True)  6 us
  transfers between devices with their start and end apart: 8, of which 5 were waited for; matrix products, arithmetic and copies ran while one was open for 13% of the time, Pallas kernels for 0%

commit v1 on v0

--- a/solution.py
+++ b/solution.py
@@ -105,7 +105,14 @@
         projected = jnp.stack(
             [jnp.concatenate(proj_re, axis=1), jnp.concatenate(proj_im, axis=1)]
         ).astype(jnp.bfloat16)
-        shard_piece = lax.all_gather(projected, "tile", axis=2, tiled=True)
+        ring = [projected]
+        for hop in range(7):
+            ring.append(lax.ppermute(ring[-1], "tile", [(dev, (dev + 1) % 8) for dev in range(8)]))
+        shard_piece = jnp.roll(
+            jnp.concatenate(ring[::-1], axis=2),
+            (lax.axis_index("tile") + 1) * ring[0].shape[2],
+            axis=2,
+        )
         term_re, term_im = complex_dot(shard_piece[0], shard_piece[1], flipped[0], flipped[1], 1)
         summed_back = jnp.stack([term_re, term_im]).astype(jnp.bfloat16)
         far_re = []

time: 294 us -> 297 us (1.010)
  blocking collectives: 98.5 us -> 67.4 us
  waiting for transfers between devices: 80.4 us -> 111 us
  starting transfers between devices: 19.5 us -> 22.9 us
    ppermute x0 -> x7, waiting for transfers between devices: none -> 36.9 us  [apply_transpose(): lax.ppermute(ring[-1], 'tile', [(dev, (dev + 1) % 8) for dev in range(8)])]
    all_gather x1 -> x0, blocking collectives: 30.7 us -> none  [apply_transpose(): shard_piece = lax.all_gather(projected, 'tile', axis=2, tiled=True)]
    ppermute x3, waiting for transfers between devices: 10.7 us -> 3.54 us  [extended(): before = lax.ppermute(last, axis, up)]
    psum x1, waiting for transfers between devices: 66.4 us -> 69.8 us  [per_device(): summed_focal = lax.psum(jnp.stack([focal_re, focal_im]), 'tile')]
  transfers between devices with their start and end apart: 8 -> 15, of which waited for: 5 -> 9; matrix products, arithmetic and copies ran while one was open for 13% -> 14% of each run, Pallas kernels for 0% -> 0%
where the time goes in v1:
time: 297 us; the launch traced here: 296 us
  waiting for transfers between devices  111 us (37%)
  blocking collectives  67.4 us (23%)
  matrix products  63.9 us (22%)
  starting transfers between devices  22.9 us (8%)
  between operations  15.4 us (5%)
  other arithmetic  8.78 us (3%)
  local copies, waits for them, and re-layouts  6.49 us (2%)
    psum x1, waiting for transfers between devices, per_device(): summed_focal = lax.psum(jnp.stack([focal_re, focal_im]), 'tile')  69.8 us
    dot_general x140, matrix products, plain_dot(): lax.dot_general(left, right, (((1,), (contract,)), ((), ())), preferred_e...  63.7 us
    all_gather x2, blocking collectives, per_device(): fold_shard_piece = lax.all_gather(coeff, 'tile', axis=2, tiled=True)  61.5 us
    ppermute x7, waiting for transfers between devices, apply_transpose(): lax.ppermute(ring[-1], 'tile', [(dev, (dev + 1) % 8) for dev in range(8)])  36.9 us
    ppermute x3, starting transfers between devices, extended(): after = lax.ppermute(initial, axis, down)  10.8 us
    all_to_all x1, starting transfers between devices, per_device(): lax.all_to_all(masked, 'tile', split_axis=1, concat_axis=2, tiled=True)  7.31 us
  transfers between devices with their start and end apart: 15, of which 9 were waited for; matrix products, arithmetic and copies ran while one was open for 14% of the time, Pallas kernels for 0%

profile of v1, /device:TPU:0, one launch (start us, length us, event | category | flops | bytes accessed | tf_op | source)
XLA Modules:
  0.0 295.5 jit_solution(5066123522385099353)
XLA Ops:
  11.9 7.3 %all-to-all-start = ((bf16[8,2,2304]{2,1,0:T(2,128)(2,1)}), bf16[8,2,2304]{2,1,0:T(2,128)(2,1)S(1)}, u32[]{:S(2)}, u32[]{:S(2)}) async-start(bf16[8,2,2304]{2,1,0:T(2,128)(2,1)} %reshape.84), calls=%async_computation | async-start | bytes 147456 | tf_op jit(solution)/shard_map/all_to_all | solution.py:66
  19.2 2.0 fusion.463
  21.3 2.0 collective-permute-start
  23.2 2.8 collective-permute-start.1
  34.5 30.6 %all_gather.6 = bf16[2,128,384]{1,2,0:T(8,128)(2,1)S(1)} all-gather(bf16[2,128,48]{1,2,0:T(8,128)(2,1)S(1)} %pad_maximum_fusion.6), channel_id=1, replica_groups=mesh['tile'=8,'src'=4] {'tile'}, dimensions={2}, use_global_device_ids=true | all-gather | bytes 221184 | tf_op jit(solution)/shard_map/all_gather | solution.py:151
  84.5 1.8 fusion.175
  87.6 1.5 fusion.20
  89.1 1.5 fusion.22
  97.1 30.9 %all_gather.7 = bf16[2,128,384]{1,2,0:T(8,128)(2,1)S(1)} all-gather(bf16[2,128,48]{1,2,0:T(8,128)(2,1)S(1)} %pad_maximum_fusion.7), channel_id=1, replica_groups=mesh['tile'=8,'src'=4] {'tile'}, dimensions={2}, use_global_device_ids=true | all-gather | bytes 221184 | tf_op jit(solution)/shard_map/all_gather | solution.py:151
  133.3 4.7 %collective-permute-start.3 = (bf16[2,128,512]{2,1,0:T(8,128)(2,1)S(1)}, bf16[2,128,512]{2,1,0:T(8,128)(2,1)S(1)}, u32[]{:S(2)}, u32[]{:S(2)}) collective-permute-start(bf16[2,128,512]{2,1,0:T(8,128)(2,1)S(1)} %get-tuple-element.10), channel_id=1, source_target_pairs={{4,0},{8,4},{12,8},{16,12},{20,16},{24,20},{28,24},{0,28},{5,1},{9... | collective-permute-start | bytes 786440 | tf_op jit(solution)/shard_map/ppermute | solution.py:19
  139.0 3.5 %collective-permute-done.2 = bf16[2,128,512]{2,1,0:T(8,128)(2,1)S(1)} collective-permute-done((bf16[2,128,512]{2,1,0:T(8,128)(2,1)S(1)}, bf16[2,128,512]{2,1,0:T(8,128)(2,1)S(1)}, u32[]{:S(2)}, u32[]{:S(2)}) %collective-permute-start.2) | collective-permute-done | bytes 262176 | tf_op jit(solution)/shard_map/ppermute | solution.py:18
  148.1 69.8 %all-reduce.2.cloned.1.call-done = f32[2,128,64]{1,2,0:T(8,128)} async-done(((f32[2,128,64]{1,2,0:T(8,128)}), f32[2,128,64]{1,2,0:T(8,128)}) %all-reduce.2.cloned.1.call-update) | async-done | bytes 65552 | tf_op jit(solution)/shard_map/psum | solution.py:196
  218.8 5.8 %psum.15 = f32[64]{0:T(128)S(1)} all-reduce(f32[64]{0:T(128)S(1)} %add_reduce_fusion), channel_id=1, replica_groups=mesh['tile'=8,'src'=4] {'src'}, use_global_device_ids=true, to_apply=%region_2.3 | all-reduce | flops 64 | bytes 512 | tf_op jit(solution)/shard_map/psum | solution.py:197
  229.9 1.4 fusion.88
  231.3 1.3 fusion.80
  236.4 1.5 collective-permute-start.6
  241.8 3.3 %collective-permute-start.5 = (bf16[2,128,512]{2,1,0:T(8,128)(2,1)S(1)}, bf16[2,128,512]{2,1,0:T(8,128)(2,1)S(1)}, u32[]{:S(2)}, u32[]{:S(2)}) collective-permute-start(bf16[2,128,512]{2,1,0:T(8,128)(2,1)S(1)} %fusion.67), channel_id=1, source_target_pairs={{4,0},{8,4},{12,8},{16,12},{20,16},{24,20},{28,24},{0,28},{5,1},{9... | collective-permute-start | bytes 786440 | tf_op jit(solution)/shard_map/ppermute | solution.py:19
  245.2 6.5 %collective-permute-done.7 = bf16[2,128,48]{1,2,0:T(8,128)(2,1)S(1)} collective-permute-done((bf16[2,128,48]{1,2,0:T(8,128)(2,1)S(1)}, bf16[2,128,48]{1,2,0:T(8,128)(2,1)S(1)}, u32[]{:S(2)}, u32[]{:S(2)}) %collective-permute-start.7) | collective-permute-done | bytes 24608 | tf_op jit(solution)/shard_map/ppermute | solution.py:110
  252.8 5.3 %collective-permute-done.8 = bf16[2,128,48]{1,2,0:T(8,128)(2,1)S(1)} collective-permute-done((bf16[2,128,48]{1,2,0:T(8,128)(2,1)S(1)}, bf16[2,128,48]{1,2,0:T(8,128)(2,1)S(1)}, u32[]{:S(2)}, u32[]{:S(2)}) %collective-permute-start.8) | collective-permute-done | bytes 24608 | tf_op jit(solution)/shard_map/ppermute | solution.py:110
  258.3 6.4 %collective-permute-done.9 = bf16[2,128,48]{1,2,0:T(8,128)(2,1)S(1)} collective-permute-done((bf16[2,128,48]{1,2,0:T(8,128)(2,1)S(1)}, bf16[2,128,48]{1,2,0:T(8,128)(2,1)S(1)}, u32[]{:S(2)}, u32[]{:S(2)}) %collective-permute-start.9) | collective-permute-done | bytes 24608 | tf_op jit(solution)/shard_map/ppermute | solution.py:110
  264.8 6.5 %collective-permute-done.10 = bf16[2,128,48]{1,2,0:T(8,128)(2,1)S(1)} collective-permute-done((bf16[2,128,48]{1,2,0:T(8,128)(2,1)S(1)}, bf16[2,128,48]{1,2,0:T(8,128)(2,1)S(1)}, u32[]{:S(2)}, u32[]{:S(2)}) %collective-permute-start.10) | collective-permute-done | bytes 24608 | tf_op jit(solution)/shard_map/ppermute | solution.py:110
  271.3 6.5 %collective-permute-done.11 = bf16[2,128,48]{1,2,0:T(8,128)(2,1)S(1)} collective-permute-done((bf16[2,128,48]{1,2,0:T(8,128)(2,1)S(1)}, bf16[2,128,48]{1,2,0:T(8,128)(2,1)S(1)}, u32[]{:S(2)}, u32[]{:S(2)}) %collective-permute-start.11) | collective-permute-done | bytes 24608 | tf_op jit(solution)/shard_map/ppermute | solution.py:110
  278.6 5.7 %collective-permute-done.12 = bf16[2,128,48]{1,2,0:T(8,128)(2,1)S(1)} collective-permute-done((bf16[2,128,48]{1,2,0:T(8,128)(2,1)S(1)}, bf16[2,128,48]{1,2,0:T(8,128)(2,1)S(1)}, u32[]{:S(2)}, u32[]{:S(2)}) %collective-permute-start.12) | collective-permute-done | bytes 24608 | tf_op jit(solution)/shard_map/ppermute | solution.py:110
  287.1 1.6 fusion.61
  (248 shorter events, 69.9 us)
Async XLA Ops:
  7.2 62.6 %copy-start.1 = (bf16[2,128,1024]{2,1,0:T(8,128)(2,1)S(1)}, bf16[2,128,1024]{2,1,0:T(8,128)(2,1)}, u32[]{:S(2)}) copy-start(bf16[2,128,1024]{2,1,0:T(8,128)(2,1)} %param.10) | copy-start | bytes 1572868
  9.8 63.8 %copy-start.2 = (bf16[2,2,24,512]{3,2,1,0:T(8,128)(2,1)S(1)}, bf16[2,2,24,512]{3,2,1,0:T(8,128)(2,1)}, u32[]{:S(2)}) copy-start(bf16[2,2,24,512]{3,2,1,0:T(8,128)(2,1)} %param.13) | copy-start | bytes 294916
  11.9 70.5 %all-to-all-start = ((bf16[8,2,2304]{2,1,0:T(2,128)(2,1)}), bf16[8,2,2304]{2,1,0:T(2,128)(2,1)S(1)}, u32[]{:S(2)}, u32[]{:S(2)}) async-start(bf16[8,2,2304]{2,1,0:T(2,128)(2,1)} %reshape.84), calls=%async_computation | async-start | bytes 147456 | tf_op jit(solution)/shard_map/all_to_all | solution.py:66
  19.2 198.8 %all-reduce.2.cloned.1.call-start = ((), (), s32[]{:S(2)}) async-start(), calls=%async_computation.1 | async-start | bytes 131072 | tf_op jit(solution)/shard_map/psum | solution.py:196
  19.2 53.1 %copy-start = (bf16[2,3,2,512,512]{4,3,2,1,0:T(8,128)(2,1)S(1)}, bf16[2,3,2,512,512]{4,3,2,1,0:T(8,128)(2,1)}, u32[]{:S(2)}) copy-start(bf16[2,3,2,512,512]{4,3,2,1,0:T(8,128)(2,1)} %param.11) | copy-start | bytes 18874372
  21.3 63.2 %collective-permute-start = (bf16[2,128,512]{2,1,0:T(8,128)(2,1)}, bf16[2,128,512]{2,1,0:T(8,128)(2,1)}, u32[]{:S(2)}, u32[]{:S(2)}) collective-permute-start(bf16[2,128,512]{2,1,0:T(8,128)(2,1)} %get-tuple-element.11), channel_id=1, source_target_pairs={{0,4},{4,8},{8,12},{12,16},{16,20},{20,24},{24,28},{28,0},{1,5},{5... | collective-permute-start | bytes 786440 | tf_op jit(solution)/shard_map/ppermute | solution.py:18
  23.2 63.0 %collective-permute-start.1 = (bf16[2,128,512]{2,1,0:T(8,128)(2,1)}, bf16[2,128,512]{2,1,0:T(8,128)(2,1)}, u32[]{:S(2)}, u32[]{:S(2)}) collective-permute-start(bf16[2,128,512]{2,1,0:T(8,128)(2,1)} %get-tuple-element.12), channel_id=1, source_target_pairs={{4,0},{8,4},{12,8},{16,12},{20,16},{24,20},{28,24},{0,28},{5,1},{9... | collective-permute-start | bytes 786440 | tf_op jit(solution)/shard_map/ppermute | solution.py:19
  77.9 14.2 %slice-start = ((s8[6291456]{0:T(1024)(128)(4,1)}), s8[2097152]{0:T(1024)(128)(4,1)S(1)}, s32[]{:S(2)}) async-start(s8[6291456]{0:T(1024)(128)(4,1)} %bitcast.613), calls=%async_computation.2 | async-start | bytes 4194304
  83.3 11.1 %copy-start.5 = (f32[128,512]{1,0:T(8,128)S(1)}, f32[128,512]{1,0:T(8,128)}, u32[]{:S(2)}) copy-start(f32[128,512]{1,0:T(8,128)} %convolution_subtract_fusion.17) | copy-start | bytes 786436
  133.3 9.2 %collective-permute-start.2 = (bf16[2,128,512]{2,1,0:T(8,128)(2,1)S(1)}, bf16[2,128,512]{2,1,0:T(8,128)(2,1)S(1)}, u32[]{:S(2)}, u32[]{:S(2)}) collective-permute-start(bf16[2,128,512]{2,1,0:T(8,128)(2,1)S(1)} %get-tuple-element.9), channel_id=1, source_target_pairs={{0,4},{4,8},{8,12},{12,16},{16,20},{20,24},{24,28},{28,0},{1,5},{5... | collective-permute-start | bytes 786440 | tf_op jit(solution)/shard_map/ppermute | solution.py:18
  133.3 9.8 %collective-permute-start.3 = (bf16[2,128,512]{2,1,0:T(8,128)(2,1)S(1)}, bf16[2,128,512]{2,1,0:T(8,128)(2,1)S(1)}, u32[]{:S(2)}, u32[]{:S(2)}) collective-permute-start(bf16[2,128,512]{2,1,0:T(8,128)(2,1)S(1)} %get-tuple-element.10), channel_id=1, source_target_pairs={{4,0},{8,4},{12,8},{16,12},{20,16},{24,20},{28,24},{0,28},{5,1},{9... | collective-permute-start | bytes 786440 | tf_op jit(solution)/shard_map/ppermute | solution.py:19
  144.1 80.5 %copy-start.10 = (f32[64]{0:T(128)S(1)}, f32[64]{0:T(128)}, u32[]{:S(2)}) copy-start(f32[64]{0:T(128)} %param.18) | copy-start | bytes 772
  145.0 87.7 %slice-start.2 = ((s8[6291456]{0:T(1024)(128)(4,1)}), s8[2097152]{0:T(1024)(128)(4,1)S(1)}, s32[]{:S(2)}) async-start(s8[6291456]{0:T(1024)(128)(4,1)} %bitcast.615), calls=%async_computation.4 | async-start | bytes 4194304
  236.4 8.7 %collective-permute-start.6 = (bf16[2,128,48]{1,2,0:T(8,128)(2,1)S(1)}, bf16[2,128,48]{1,2,0:T(8,128)(2,1)S(1)}, u32[]{:S(2)}, u32[]{:S(2)}) collective-permute-start(bf16[2,128,48]{1,2,0:T(8,128)(2,1)S(1)} %pad_maximum_fusion.8), channel_id=1, source_target_pairs={{0,4},{4,8},{8,12},{12,16},{16,20},{20,24},{24,28},{28,0},{1,5},{5... | collective-permute-start | bytes 73736 | tf_op jit(solution)/shard_map/ppermute | solution.py:110
  240.7 37.0 %copy-start.11 = (s32[64]{0:T(128)S(1)}, s32[64]{0:T(128)}, u32[]{:S(2)}) copy-start(s32[64]{0:T(128)} %param.19) | copy-start | bytes 772
  241.1 43.9 %copy-start.9 = (bf16[2,2,24,512]{3,2,1,0:T(8,128)(2,1)S(1)}, bf16[2,2,24,512]{3,2,1,0:T(8,128)(2,1)}, u32[]{:S(2)}) copy-start(bf16[2,2,24,512]{3,2,1,0:T(8,128)(2,1)} %param.12) | copy-start | bytes 294916
  241.8 45.2 %collective-permute-start.5 = (bf16[2,128,512]{2,1,0:T(8,128)(2,1)S(1)}, bf16[2,128,512]{2,1,0:T(8,128)(2,1)S(1)}, u32[]{:S(2)}, u32[]{:S(2)}) collective-permute-start(bf16[2,128,512]{2,1,0:T(8,128)(2,1)S(1)} %fusion.67), channel_id=1, source_target_pairs={{4,0},{8,4},{12,8},{16,12},{20,16},{24,20},{28,24},{0,28},{5,1},{9... | collective-permute-start | bytes 786440 | tf_op jit(solution)/shard_map/ppermute | solution.py:19
  245.1 6.5 %collective-permute-start.7 = (bf16[2,128,48]{1,2,0:T(8,128)(2,1)S(1)}, bf16[2,128,48]{1,2,0:T(8,128)(2,1)S(1)}, u32[]{:S(2)}, u32[]{:S(2)}) collective-permute-start(bf16[2,128,48]{1,2,0:T(8,128)(2,1)S(1)} %collective-permute-done.6), channel_id=1, source_target_pairs={{0,4},{4,8},{8,12},{12,16},{16,20},{20,24},{24,28},{28,0},{1,5},{5... | collective-permute-start | bytes 73736 | tf_op jit(solution)/shard_map/ppermute | solution.py:110
  251.7 6.5 %collective-permute-start.8 = (bf16[2,128,48]{1,2,0:T(8,128)(2,1)S(1)}, bf16[2,128,48]{1,2,0:T(8,128)(2,1)S(1)}, u32[]{:S(2)}, u32[]{:S(2)}) collective-permute-start(bf16[2,128,48]{1,2,0:T(8,128)(2,1)S(1)} %collective-permute-done.7), channel_id=1, source_target_pairs={{0,4},{4,8},{8,12},{12,16},{16,20},{20,24},{24,28},{28,0},{1,5},{5... | collective-permute-start | bytes 73736 | tf_op jit(solution)/shard_map/ppermute | solution.py:110
  258.2 6.5 %collective-permute-start.9 = (bf16[2,128,48]{1,2,0:T(8,128)(2,1)S(1)}, bf16[2,128,48]{1,2,0:T(8,128)(2,1)S(1)}, u32[]{:S(2)}, u32[]{:S(2)}) collective-permute-start(bf16[2,128,48]{1,2,0:T(8,128)(2,1)S(1)} %collective-permute-done.8), channel_id=1, source_target_pairs={{0,4},{4,8},{8,12},{12,16},{16,20},{20,24},{24,28},{28,0},{1,5},{5... | collective-permute-start | bytes 73736 | tf_op jit(solution)/shard_map/ppermute | solution.py:110
  258.2 28.8 %collective-permute-start.4 = (bf16[2,128,512]{2,1,0:T(8,128)(2,1)S(1)}, bf16[2,128,512]{2,1,0:T(8,128)(2,1)S(1)}, u32[]{:S(2)}, u32[]{:S(2)}) collective-permute-start(bf16[2,128,512]{2,1,0:T(8,128)(2,1)S(1)} %fusion.69), channel_id=1, source_target_pairs={{0,4},{4,8},{8,12},{12,16},{16,20},{20,24},{24,28},{28,0},{1,5},{5... | collective-permute-start | bytes 786440 | tf_op jit(solution)/shard_map/ppermute | solution.py:18
  264.7 6.5 %collective-permute-start.10 = (bf16[2,128,48]{1,2,0:T(8,128)(2,1)S(1)}, bf16[2,128,48]{1,2,0:T(8,128)(2,1)S(1)}, u32[]{:S(2)}, u32[]{:S(2)}) collective-permute-start(bf16[2,128,48]{1,2,0:T(8,128)(2,1)S(1)} %collective-permute-done.9), channel_id=1, source_target_pairs={{0,4},{4,8},{8,12},{12,16},{16,20},{20,24},{24,28},{28,0},{1,5},{5... | collective-permute-start | bytes 73736 | tf_op jit(solution)/shard_map/ppermute | solution.py:110
  271.2 6.5 %collective-permute-start.11 = (bf16[2,128,48]{1,2,0:T(8,128)(2,1)S(1)}, bf16[2,128,48]{1,2,0:T(8,128)(2,1)S(1)}, u32[]{:S(2)}, u32[]{:S(2)}) collective-permute-start(bf16[2,128,48]{1,2,0:T(8,128)(2,1)S(1)} %collective-permute-done.10), channel_id=1, source_target_pairs={{0,4},{4,8},{8,12},{12,16},{16,20},{20,24},{24,28},{28,0},{1,5},{5... | collective-permute-start | bytes 73736 | tf_op jit(solution)/shard_map/ppermute | solution.py:110
  277.8 6.5 %collective-permute-start.12 = (bf16[2,128,48]{1,2,0:T(8,128)(2,1)S(1)}, bf16[2,128,48]{1,2,0:T(8,128)(2,1)S(1)}, u32[]{:S(2)}, u32[]{:S(2)}) collective-permute-start(bf16[2,128,48]{1,2,0:T(8,128)(2,1)S(1)} %collective-permute-done.11), channel_id=1, source_target_pairs={{0,4},{4,8},{8,12},{12,16},{16,20},{20,24},{24,28},{28,0},{1,5},{5... | collective-permute-start | bytes 73736 | tf_op jit(solution)/shard_map/ppermute | solution.py:110
  (7 other events, 58.3 us)
Sparse Core Ops, SparseCore 0:
  147.9 69.9 all-reduce.1
